TPU v7x, 32 devices: a whole 2x2x4 slice. The times are simulated.
32 devices in a mesh: row: 4 (over x, core), col: 8 (over z, y).
Axes of the slice: x: 2, y: 2, z: 4, core: 2. Of those that a mesh axis runs over, the one named last changes fastest.
Arguments:
- ground_level_map: float32 [512, 4096], P('row', 'col'), may hold values from 0 to 10
- shoreline_altitude_entries: float32 [32768, 128], P(('row', 'col')), may hold values from 2 to 14
- shoreline_piece_position: int32 [32768], P(('row', 'col')), may hold values from 0 to 511
- lake_panel_locations: float32 [512, 2, 512], P(('row', 'col')), may hold values from 0 to 4096, as said below
- spanned_patch_verticals: int32 [512, 2], P(('row', 'col')), may hold values from 0 to 7, all different within a row; in each aligned block of 16 rows (0 to 15, 16 to 31, ...) at most 6 rows name the same one
Outputs:
- depth: float32 [512, 4096], P('row', 'col')
Inputs may be any that keep to these rules, and one draw needn't show every extreme that they name: shoreline_piece_position // 4 numbers a water body of the record's own tile row. `spanned_patch_verticals`: each body names 2 different tile columns; among the 16 bodies of one device no tile column is named more than 6 times, and some device's bodies name some column exactly 6 times. `lake_panel_locations`: entry 0 of a point is a row coordinate inside the rows of the body's tile row, entry 1 a column coordinate of the grid.
All inputs are finite; a program needn't handle non-finite values.
Results may differ from a plain program's by a relative error of at most 0.0003.
Values sent between devices are 32-bit elements; how exact they have to be, the bound alone decides.
No kernel may reach another device: no remote copies, remote signals or barrier semaphores. Data moves between devices by JAX's collectives and lax.ppermute only.
A program may use at most 64 MiB of HBM per device.

v0:
```python
import functools

import jax
import jax.numpy as jnp
from jax import lax
from jax.experimental import pallas as pl
from jax.experimental.pallas import tpu as pltpu
from jax.sharding import PartitionSpec as P

SEGS = 4
SWEEPS = 4
MOST = 6
LANES = 128

spread = 4.0
tau_weight = 4.0
flow_gain = 8.0

F32 = jnp.float32
BF16 = jnp.bfloat16
VMEM_LIMIT = 24 * 1024 * 1024


def vmem():
    return pl.BlockSpec(memory_space=pltpu.VMEM)


def smem():
    return pl.BlockSpec(memory_space=pltpu.SMEM)


def params(limit=VMEM_LIMIT):
    return pltpu.CompilerParams(vmem_limit_bytes=limit)


def one_hot(cond):
    return jnp.where(cond, 1.0, 0.0).astype(BF16)


def pack_kernel(
    cover_hbm,
    ids_hbm,
    entry_hbm,
    place_hbm,
    ground_hbm,
    out_ref,
    ground_ref,
    cover_copy_ref,
    cover_ref,
    ids_ref,
    entry_ref,
    place_ref,
    used_ref,
    sems,
):
    owners, _, _ = out_ref.shape
    covers, bodies = cover_ref.shape
    copies = [
        pltpu.make_async_copy(source, target, sems.at[k])
        for k, (source, target) in enumerate(
            (
                (ids_hbm, ids_ref),
                (entry_hbm, entry_ref),
                (place_hbm, place_ref),
                (cover_hbm, cover_ref),
                (cover_hbm, cover_copy_ref),
                (ground_hbm, ground_ref),
            )
        )
    ]
    for copy in copies:
        copy.start()
    chunks = ids_ref.shape[0]
    sum_rows, count_rows = bodies * SEGS, bodies // 2
    first_slot = sum_rows + count_rows
    out_ref[:, first_slot:, :] = jnp.zeros((owners, MOST * 8, LANES), F32)
    for copy in copies:
        copy.wait()
    seg_iota = lax.broadcasted_iota(jnp.int32, (owners * sum_rows, LANES), 0)
    pair_iota = lax.broadcasted_iota(jnp.int32, (owners * count_rows, LANES), 0)
    lane_group = lax.broadcasted_iota(jnp.int32, (LANES, LANES), 0) // 16
    ids = [ids_ref[k : k + 1, :] for k in range(chunks)]
    by_pair = jnp.concatenate([one_hot(pair_iota == v // 8) for v in ids], axis=1)
    by_lane = jnp.concatenate([one_hot(lane_group == v % 8) for v in ids], axis=1)
    counts = lax.dot_general(
        by_pair, by_lane, (((1,), (1,)), ((), ())), preferred_element_type=F32
    )
    by_segment = jnp.concatenate([one_hot(seg_iota == v) for v in ids], axis=1)
    entries = entry_ref[...]
    high = entries.astype(BF16)
    low = (entries - high.astype(F32)).astype(BF16)
    both = jnp.dot(
        by_segment, jnp.concatenate([high, low], axis=1), preferred_element_type=F32
    )
    sums = both[:, :LANES] + both[:, LANES:]
    for owner in range(owners):
        out_ref[owner, :sum_rows, :] = sums[owner * sum_rows : (owner + 1) * sum_rows]
        out_ref[owner, sum_rows:first_slot, :] = counts[
            owner * count_rows : (owner + 1) * count_rows
        ]
    for column in range(owners):
        used_ref[column] = 0
    for body_id in range(bodies):
        rows = place_ref[body_id]
        tile = jnp.concatenate(
            [
                rows[axis : axis + 1, s * LANES : (s + 1) * LANES]
                for axis in range(2)
                for s in range(SEGS)
            ],
            axis=0,
        )
        for k in range(covers):
            column = cover_ref[k, body_id]
            slot = used_ref[column]
            used_ref[column] = slot + 1
            out_ref[column, pl.ds(pl.multiple_of(first_slot + slot * 8, 8), 8), :] = tile


def owner_kernel(cover_ref, part_ref, out_ref, total_ref, used_ref):
    columns = out_ref.shape[0]
    covers, bodies = cover_ref.shape
    rows = total_ref.shape[0]
    total = part_ref[0, :rows, :]
    for source in range(1, part_ref.shape[0]):
        total = total + part_ref[source, :rows, :]
    total_ref[...] = total
    out_ref[...] = jnp.zeros_like(out_ref)
    for column in range(columns):
        used_ref[column] = 0
    for body_id in range(bodies):
        sums = total_ref[body_id * SEGS : (body_id + 1) * SEGS, :]
        row, lane = bodies * SEGS + body_id // 2, 64 * (body_id % 2)
        count = total_ref[row : row + 1, lane : lane + 64]
        for k in range(covers):
            column = cover_ref[k, body_id]
            slot = used_ref[column]
            used_ref[column] = slot + 1
            out_ref[column, pl.ds(slot * SEGS, SEGS), :] = sums
            out_ref[column, pl.ds(MOST * SEGS + slot, 1), :64] = count
    for column in range(columns):
        out_ref[column, MOST * SEGS + MOST : MOST * SEGS + MOST + 1, :] = jnp.full(
            (1, LANES), used_ref[column].astype(F32), F32
        )


def lorentz(base, step):
    distance = base + step
    return 1.0 / (1.0 + distance * distance)


def cell_base(origin, coord):
    index = lax.broadcasted_iota(jnp.int32, (16, LANES), 0).astype(F32) * (1.0 / spread)
    return index - (coord - origin) * (1.0 / spread)


def column_block(place_ref, owner, row, origin, starts):
    parts = []
    for s in range(SEGS):
        base = cell_base(origin, place_ref[owner, row + SEGS + s : row + SEGS + s + 1, :])
        parts.append(
            jnp.concatenate(
                [
                    lorentz(base, (start + j) / spread).astype(BF16)
                    for start in starts
                    for j in range(0, LANES, 16)
                ],
                axis=0,
            )
        )
    return jnp.concatenate(parts, axis=1)


def times_stack(columns, stack):
    return lax.dot_general(
        columns, stack, (((1,), (1,)), ((), ())), preferred_element_type=F32
    )


def surface(acc, mean, ground):
    tile_rows = ground.shape[0]
    num = jnp.transpose(acc[:, :tile_rows])
    den = jnp.transpose(acc[:, tile_rows:])
    depth = (num + (mean - ground) * den) / (den + tau_weight)
    return jnp.maximum(depth, 0.0)


def for_used_slots(owners, codes, run):
    for group, code in enumerate(codes):

        @pl.loop(0, min(8, owners - 8 * group))
        def _(k):
            used = lax.shift_right_logical(code, 3 * k) & 7
            for slots in range(2, MOST + 1, 2):

                @pl.when((used <= slots) & (used > slots - 2))
                def _():
                    run(8 * group + k, slots)


def outer_kernel(
    first_slot, place_ref, sums_ref, ground_ref, depth_ref, left_ref, right_ref, stack_ref, mean_ref, acc_ref
):
    tile_rows, tile_columns = ground_ref.shape
    owners = sums_ref.shape[0]
    row_origin = (lax.axis_index("row") * tile_rows).astype(F32)
    col_origin = (lax.axis_index("col") * tile_columns).astype(F32)
    elev = jnp.sum(sums_ref[:, : MOST * SEGS, :], axis=0)
    count = jnp.sum(sums_ref[:, MOST * SEGS : MOST * SEGS + MOST, :], axis=0)
    elev = jnp.sum(jnp.sum(elev, axis=0, keepdims=True), axis=1, keepdims=True)
    count = jnp.sum(jnp.sum(count, axis=0, keepdims=True), axis=1, keepdims=True)
    mean = elev / jnp.maximum(count * (LANES / 16), 1.0)
    mean_ref[...] = jnp.broadcast_to(mean, mean_ref.shape)
    codes = []
    for group in range((owners + 7) // 8):
        code = jnp.zeros((1, 1), F32)
        for owner in range(8 * group, min(8 * group + 8, owners)):
            used = sums_ref[owner, MOST * SEGS + MOST : MOST * SEGS + MOST + 1, 0:1]
            code = code + used * (8.0 ** (owner % 8))
        mean_ref[group + 1 : group + 2, :] = jnp.broadcast_to(code, (1, LANES))
        codes.append(jnp.max(code).astype(jnp.int32))
    acc_ref[...] = jnp.zeros_like(acc_ref)
    starts = (0, tile_columns - LANES)

    def run(owner, slots):
        for slot in range(slots):
            row = first_slot + slot * 8
            blocks = []
            for s in range(SEGS):
                here = sums_ref[owner, MOST * SEGS + slot : MOST * SEGS + slot + 1, s * 16 : s * 16 + 1]
                part = sums_ref[owner, slot * SEGS + s : slot * SEGS + s + 1, :] - mean * here
                weight = jnp.broadcast_to(here, (16, LANES))
                part = jnp.broadcast_to(part, (16, LANES))
                base = cell_base(row_origin, place_ref[owner, row + s : row + s + 1, :])
                values = [lorentz(base, i / spread) for i in range(0, tile_rows, 16)]
                block = jnp.concatenate(
                    [(v * part).astype(BF16) for v in values]
                    + [(v * weight).astype(BF16) for v in values],
                    axis=0,
                )
                stack_ref[owner * (MOST * SEGS) + slot * SEGS + s] = block
                blocks.append(block)
            columns = column_block(place_ref, owner, row, col_origin, starts)
            acc_ref[...] += times_stack(columns, jnp.concatenate(blocks, axis=1))

    for_used_slots(owners, codes, run)
    ground = jnp.concatenate(
        [ground_ref[:, start : start + LANES] for start in starts], axis=1
    )
    depth = surface(acc_ref[...], mean, ground)
    depth_ref[...] = depth
    for out_ref, start, pick in ((left_ref, 0, 0), (right_ref, LANES, LANES - SWEEPS)):
        for k, values in enumerate((depth, ground)):
            out_ref[k * SWEEPS : (k + 1) * SWEEPS, :] = jnp.transpose(
                values[:, start : start + LANES]
            )[pick : pick + SWEEPS]


def inner_kernel(first_slot, place_ref, stack_ref, mean_ref, ground_ref, depth_ref, acc_ref):
    tile_columns = ground_ref.shape[1]
    owners = place_ref.shape[0]
    col_origin = (lax.axis_index("col") * tile_columns).astype(F32)
    acc_ref[...] = jnp.zeros_like(acc_ref)
    starts = tuple(range(LANES, tile_columns - LANES, LANES))
    codes = [
        jnp.max(mean_ref[group + 1 : group + 2, :]).astype(jnp.int32)
        for group in range((owners + 7) // 8)
    ]

    def run(owner, slots):
        for slot in range(slots):
            columns = column_block(place_ref, owner, first_slot + slot * 8, col_origin, starts)
            stack = jnp.concatenate(
                [stack_ref[owner * (MOST * SEGS) + slot * SEGS + s] for s in range(SEGS)], axis=1
            )
            acc_ref[...] += times_stack(columns, stack)

    for_used_slots(owners, codes, run)
    ground = ground_ref[:, LANES : tile_columns - LANES]
    depth_ref[...] = surface(acc_ref[...], mean_ref[0:1, 0:1], ground)


def extend_kernel(
    outer_ref, inner_ref, ground_ref, left_ref, right_ref, height_ref, land_ref, top_ref, bottom_ref
):
    tile_rows, tile_columns = ground_ref.shape
    sides = jnp.transpose(jnp.concatenate([left_ref[...], right_ref[...]], axis=0))
    blank = jnp.zeros((tile_rows, LANES - 2 * SWEEPS), F32)
    height_ref[:, :LANES] = outer_ref[:, :LANES]
    height_ref[:, LANES : tile_columns - LANES] = inner_ref[...]
    height_ref[:, tile_columns - LANES : tile_columns] = outer_ref[:, LANES:]
    land_ref[:, :tile_columns] = ground_ref[...]
    for k, ref in enumerate((height_ref, land_ref)):
        left = sides[:, k * SWEEPS : (k + 1) * SWEEPS]
        right = sides[:, (2 + k) * SWEEPS : (3 + k) * SWEEPS]
        ref[:, tile_columns:] = jnp.concatenate([right, blank, left], axis=1)
        rows = slice(k * SWEEPS, (k + 1) * SWEEPS)
        top_ref[rows, :] = ref[:SWEEPS, :]
        bottom_ref[rows, :] = ref[tile_rows - SWEEPS :, :]


def relax(height, land, row_id, row_count, col_count, tile_rows, tile_columns):
    rows, cols = height.shape
    row_id = row_id + lax.axis_index("row") * tile_rows
    col_id = lax.broadcasted_iota(jnp.int32, (1, cols), 1)
    col_id = jnp.where(col_id < tile_columns + LANES // 2, col_id, col_id - cols)
    col_id = col_id + lax.axis_index("col") * tile_columns
    grid_rows, grid_cols = tile_rows * row_count, tile_columns * col_count
    gain_down = jnp.where((row_id >= 0) & (row_id < grid_rows - 1), flow_gain, 0.0)
    gain_right = jnp.where((col_id >= 0) & (col_id < grid_cols - 1), flow_gain, 0.0)
    down = gain_down / (1.0 + jnp.abs(land - pltpu.roll(land, rows - 1, 0)))
    right = gain_right / (1.0 + jnp.abs(land - pltpu.roll(land, cols - 1, 1)))
    up = pltpu.roll(down, 1, 0)
    left = pltpu.roll(right, 1, 1)
    scale = 1.0 / (1.0 + up + down + left + right)
    up, down, left, right = up * scale, down * scale, left * scale, right * scale
    for _ in range(SWEEPS):
        height = (
            height * scale
            + up * pltpu.roll(height, 1, 0)
            + down * pltpu.roll(height, rows - 1, 0)
            + left * pltpu.roll(height, 1, 1)
            + right * pltpu.roll(height, cols - 1, 1)
        )
    return height


def middle_kernel(row_count, col_count, height_ref, land_ref, out_ref):
    tile_rows, tile_columns = out_ref.shape
    row_id = lax.broadcasted_iota(jnp.int32, (tile_rows, 1), 0)
    height = relax(
        height_ref[...], land_ref[...], row_id, row_count, col_count, tile_rows, tile_columns
    )
    out_ref[...] = height[:, :tile_columns]


def band_kernel(row_count, col_count, height_ref, land_ref, above_ref, below_ref, _, out_hbm, rows_ref, sems):
    tile_rows, tile_columns = out_hbm.shape
    keep = 16 - SWEEPS

    def bands(ref, k):
        halo = slice(k * SWEEPS, (k + 1) * SWEEPS)
        return jnp.concatenate(
            [above_ref[halo, :], ref[:keep, :], ref[tile_rows - keep :, :], below_ref[halo, :]],
            axis=0,
        )

    row_id = lax.broadcasted_iota(jnp.int32, (32, 1), 0)
    row_id = jnp.where(row_id < 16, row_id - SWEEPS, row_id - 16 + tile_rows - keep)
    height = relax(
        bands(height_ref, 0), bands(land_ref, 1), row_id, row_count, col_count, tile_rows, tile_columns
    )
    rows_ref[0] = height[SWEEPS : SWEEPS + 8, :tile_columns]
    rows_ref[1] = height[16 + SWEEPS : 24 + SWEEPS, :tile_columns]
    copies = [
        pltpu.make_async_copy(rows_ref.at[k], out_hbm.at[pl.ds(first, 8), :], sems.at[k])
        for k, first in enumerate((0, tile_rows - 8))
    ]
    for copy in copies:
        copy.start()
    for copy in copies:
        copy.wait()


def shift(values, axis, step):
    count = lax.axis_size(axis)
    return lax.ppermute(values, axis, [(i, (i + step) % count) for i in range(count)])


def body(
    ground_level_map,
    shoreline_altitude_entries,
    shoreline_piece_position,
    lake_panel_locations,
    spanned_patch_verticals,
):
    tile_rows, tile_columns = ground_level_map.shape
    col_count = lax.axis_size("col")
    row_count = lax.axis_size("row")
    records, _ = shoreline_altitude_entries.shape
    bodies, _ = spanned_patch_verticals.shape
    covers = spanned_patch_verticals.T
    first_slot = bodies * SEGS + bodies // 2
    hbm = pl.BlockSpec(memory_space=pltpu.HBM)

    parts, ground_level_map, covers = pl.pallas_call(
        pack_kernel,
        out_shape=(
            jax.ShapeDtypeStruct((col_count, first_slot + MOST * 8, LANES), F32),
            jax.ShapeDtypeStruct(ground_level_map.shape, F32),
            jax.ShapeDtypeStruct(covers.shape, jnp.int32),
        ),
        in_specs=[hbm] * 5,
        out_specs=(vmem(),) * 3,
        scratch_shapes=[
            pltpu.SMEM(covers.shape, jnp.int32),
            pltpu.VMEM((records // LANES, LANES), jnp.int32),
            pltpu.VMEM((records, LANES), F32),
            pltpu.VMEM(lake_panel_locations.shape, F32),
            pltpu.SMEM((col_count,), jnp.int32),
            pltpu.SemaphoreType.DMA((6,)),
        ],
        compiler_params=params(),
    )(
        *(
            pltpu.with_memory_space_constraint(value, pltpu.HBM)
            for value in (
                covers,
                shoreline_piece_position.reshape(records // LANES, LANES),
                shoreline_altitude_entries,
                lake_panel_locations,
                ground_level_map,
            )
        )
    )
    parts = lax.all_to_all(parts, "col", 0, 0, tiled=True)

    slot_rows = MOST * SEGS + 8
    sums = pl.pallas_call(
        owner_kernel,
        out_shape=jax.ShapeDtypeStruct((col_count, slot_rows, LANES), F32),
        in_specs=[smem(), vmem()],
        out_specs=vmem(),
        scratch_shapes=[
            pltpu.VMEM((first_slot, LANES), F32),
            pltpu.SMEM((col_count,), jnp.int32),
        ],
        compiler_params=params(),
    )(covers, parts)
    sums = lax.all_to_all(sums, "col", 0, 0, tiled=True)

    half = 2 * LANES
    blocks = col_count * MOST * SEGS
    flops = 4 * tile_rows * half * blocks * LANES
    edge = jax.ShapeDtypeStruct((2 * SWEEPS, tile_rows), F32)
    outer, left, right, stack, mean = pl.pallas_call(
        functools.partial(outer_kernel, first_slot),
        out_shape=(
            jax.ShapeDtypeStruct((tile_rows, half), F32),
            edge,
            edge,
            jax.ShapeDtypeStruct((blocks, 2 * tile_rows, LANES), BF16),
            jax.ShapeDtypeStruct((8, LANES), F32),
        ),
        in_specs=[vmem()] * 3,
        out_specs=(vmem(),) * 5,
        scratch_shapes=[pltpu.VMEM((half, 2 * tile_rows), F32)],
        compiler_params=params(),
        cost_estimate=pl.CostEstimate(flops=flops, transcendentals=0, bytes_accessed=1 << 20),
    )(parts, sums, ground_level_map)
    from_left = shift(right, "col", 1)
    from_right = shift(left, "col", -1)
    inside = tile_columns - half
    inner = pl.pallas_call(
        functools.partial(inner_kernel, first_slot),
        out_shape=jax.ShapeDtypeStruct((tile_rows, inside), F32),
        in_specs=[vmem()] * 4,
        out_specs=vmem(),
        scratch_shapes=[pltpu.VMEM((inside, 2 * tile_rows), F32)],
        compiler_params=params(),
        cost_estimate=pl.CostEstimate(flops=flops, transcendentals=0, bytes_accessed=1 << 20),
    )(parts, stack, mean, ground_level_map)

    wide = jax.ShapeDtypeStruct((tile_rows, tile_columns + LANES), F32)
    edge = jax.ShapeDtypeStruct((2 * SWEEPS, tile_columns + LANES), F32)
    height, land, top, bottom = pl.pallas_call(
        extend_kernel,
        out_shape=(wide, wide, edge, edge),
        in_specs=[vmem()] * 5,
        out_specs=(vmem(),) * 4,
        compiler_params=params(),
    )(outer, inner, ground_level_map, from_left, from_right)
    from_above = shift(bottom, "row", 1)
    from_below = shift(top, "row", -1)
    tile = jax.ShapeDtypeStruct((tile_rows, tile_columns), F32)
    depth = pl.pallas_call(
        functools.partial(middle_kernel, row_count, col_count),
        out_shape=tile,
        in_specs=[vmem()] * 2,
        out_specs=vmem(),
        compiler_params=params(),
        cost_estimate=pl.CostEstimate(
            flops=100 * tile_rows * tile_columns, transcendentals=0, bytes_accessed=1 << 22
        ),
    )(height, land)
    return pl.pallas_call(
        functools.partial(band_kernel, row_count, col_count),
        out_shape=tile,
        in_specs=[vmem()] * 4 + [hbm],
        out_specs=hbm,
        input_output_aliases={4: 0},
        scratch_shapes=[pltpu.VMEM((2, 8, tile_columns), F32), pltpu.SemaphoreType.DMA((2,))],
        compiler_params=params(),
    )(height, land, from_above, from_below, depth)


def solution(mesh):
    in_specs = (
        P("row", "col"),
        P(("row", "col"), None),
        P(("row", "col")),
        P(("row", "col"), None, None),
        P(("row", "col"), None),
    )
    out_specs = P("row", "col")
    return jax.shard_map(body, mesh=mesh, in_specs=in_specs, out_specs=out_specs, check_vma=False)
```

profile of v0, /device:TPU:9, one launch (start us, length us, event | category | flops | bytes accessed | tf_op | source)
XLA Modules:
  0.0 54.9 jit_solution(10025172190685103185)
XLA Ops:
  0.0 1.8 %shard_map.55 = (f32[8,120,128]{2,1,0:T(8,128)S(1)}, f32[128,512]{1,0:T(8,128)S(1)}, s32[2,16]{1,0:T(2,128)S(1)}) custom-call(s32[2,16]{1,0:T(2,128)} %bitcast.3, s32[8,128]{1,0:T(8,128)} %bitcast.2, f32[1024,128]{1,0:T(8,128)} %entry_hbm.1, f32[16,2,512]{2,1,0:T(2,128)} %place_hbm.1, f32[128,512]{1,0:T(8,128)} %ground_hbm.1), custom_call_target="tpu_custom_call" | custom-call | tf_op jit(solution)/shard_map/pallas_call | solution.py:386
  1.8 17.6 %all_to_all.10.part_ref.place_ref = f32[8,120,128]{2,1,0:T(8,128)S(1)} all-to-all(f32[8,120,128]{2,1,0:T(8,128)S(1)} %get-tuple-element.17), channel_id=1, replica_groups=mesh['row'=4,'col'=8] {'col'}, dimensions={0} | all-to-all | bytes 983040 | tf_op jit(solution)/shard_map/all_to_all | solution.py:416
  19.4 0.7 %shard_map.56 = f32[8,32,128]{2,1,0:T(8,128)S(1)} custom-call(s32[2,16]{1,0:T(2,128)S(1)} %get-tuple-element.18.cover_ref, f32[8,120,128]{2,1,0:T(8,128)S(1)} %all_to_all.10.part_ref.place_ref), custom_call_target="tpu_custom_call" | custom-call | tf_op jit(solution)/shard_map/pallas_call | solution.py:419
  20.1 9.2 %all_to_all.11.sums_ref = f32[8,32,128]{2,1,0:T(8,128)S(1)} all-to-all(f32[8,32,128]{2,1,0:T(8,128)S(1)} %shard_map.56), channel_id=1, replica_groups=mesh['row'=4,'col'=8] {'col'}, dimensions={0} | all-to-all | bytes 262144 | tf_op jit(solution)/shard_map/all_to_all | solution.py:430
  29.3 8.7 %shard_map.57 = (f32[128,256]{1,0:T(8,128)S(1)}, f32[8,128]{1,0:T(8,128)S(1)}, f32[8,128]{1,0:T(8,128)S(1)}, bf16[192,256,128]{2,1,0:T(8,128)(2,1)S(1)}, f32[8,128]{1,0:T(8,128)S(1)}) custom-call(f32[8,120,128]{2,1,0:T(8,128)S(1)} %all_to_all.10.part_ref.place_ref, f32[8,32,128]{2,1,0:T(8,128)S(1)} %all_to_all.11.sums_ref, ...), custom_call_target="tpu_custom_call" | custom-call | flops 3221225472 | bytes 1048576 | tf_op jit(solution)/shard_map/pallas_call | solution.py:436
  38.1 0.1 collective-permute-start
  38.1 2.4 %collective-permute-start.1 = (f32[8,128]{1,0:T(8,128)S(1)}, f32[8,128]{1,0:T(8,128)S(1)}, u32[]{:S(2)}, u32[]{:S(2)}) collective-permute-start(f32[8,128]{1,0:T(8,128)S(1)} %get-tuple-element.24), channel_id=1, source_target_pairs={{0,7},{1,0},{2,1},{3,2},{4,3},{5,4},{6,5},{7,6},{8,15},{9,8},{10,9... | collective-permute-start | bytes 12296 | tf_op jit(solution)/shard_map/ppermute | solution.py:367
  40.5 5.7 %shard_map.58.inner_ref = f32[128,256]{1,0:T(8,128)S(1)} custom-call(f32[8,120,128]{2,1,0:T(8,128)S(1)} %all_to_all.10.part_ref.place_ref, bf16[192,256,128]{2,1,0:T(8,128)(2,1)S(1)} %get-tuple-element.21.stack_ref, f32[8,128]{1,0:T(8,128)S(1)} %get-tuple-element.22.mean_ref, f32[128,512]{1,0:T(8,128)S(1)} %get-tuple-element.19.ground_ref), custom_call_target="tpu_custom_call" | custom-call | flops 3221225472 | bytes 1048576 | tf_op jit(solution)/shard_map/pallas_call | solution.py:454
  46.2 0.0 collective-permute-done.left_ref
  46.2 0.0 collective-permute-done.1.right_ref
  46.3 0.2 shard_map.59
  46.5 4.1 %collective-permute-start.2 = (f32[8,640]{1,0:T(8,128)S(1)}, f32[8,640]{1,0:T(8,128)S(1)}, u32[]{:S(2)}, u32[]{:S(2)}) collective-permute-start(f32[8,640]{1,0:T(8,128)S(1)} %get-tuple-element.27), channel_id=1, source_target_pairs={{0,8},{8,16},{16,24},{24,0},{1,9},{9,17},{17,25},{25,1},{2,10},{10... | collective-permute-start | bytes 61448 | tf_op jit(solution)/shard_map/ppermute | solution.py:367
  50.5 0.0 collective-permute-start.3
  50.5 1.8 %shard_map.60._ = f32[128,512]{1,0:T(8,128)} custom-call(f32[128,640]{1,0:T(8,128)S(1)} %get-tuple-element.25.height_ref, f32[128,640]{1,0:T(8,128)S(1)} %get-tuple-element.26.land_ref), custom_call_target="tpu_custom_call" | custom-call | flops 6553600 | bytes 4194304 | tf_op jit(solution)/shard_map/pallas_call | solution.py:476
  52.3 0.0 collective-permute-done.2.above_ref
  52.3 1.4 %collective-permute-done.3.below_ref = f32[8,640]{1,0:T(8,128)S(1)} collective-permute-done((f32[8,640]{1,0:T(8,128)S(1)}, f32[8,640]{1,0:T(8,128)S(1)}, u32[]{:S(2)}, u32[]{:S(2)}) %collective-permute-start.3) | collective-permute-done | bytes 20512 | tf_op jit(solution)/shard_map/ppermute | solution.py:367
  53.7 1.1 %shard_map.61 = f32[128,512]{1,0:T(8,128)} custom-call(f32[128,640]{1,0:T(8,128)S(1)} %get-tuple-element.25.height_ref, f32[128,640]{1,0:T(8,128)S(1)} %get-tuple-element.26.land_ref, f32[8,640]{1,0:T(8,128)S(1)} %collective-permute-done.2.above_ref, f32[8,640]{1,0:T(8,128)S(1)} %collective-permute-done.3.below_ref, ...), custom_call_target="tpu_custom_call", output_to_operand_aliasing={{}: (4, {})} | custom-call | tf_op jit(solution)/shard_map/pallas_call | solution.py:486
Async XLA Ops:
  38.1 8.2 %collective-permute-start = (f32[8,128]{1,0:T(8,128)S(1)}, f32[8,128]{1,0:T(8,128)S(1)}, u32[]{:S(2)}, u32[]{:S(2)}) collective-permute-start(f32[8,128]{1,0:T(8,128)S(1)} %get-tuple-element.23), channel_id=1, source_target_pairs={{0,1},{1,2},{2,3},{3,4},{4,5},{5,6},{6,7},{7,0},{8,9},{9,10},{10,1... | collective-permute-start | bytes 12296 | tf_op jit(solution)/shard_map/ppermute | solution.py:367
  38.1 8.1 %collective-permute-start.1 = (f32[8,128]{1,0:T(8,128)S(1)}, f32[8,128]{1,0:T(8,128)S(1)}, u32[]{:S(2)}, u32[]{:S(2)}) collective-permute-start(f32[8,128]{1,0:T(8,128)S(1)} %get-tuple-element.24), channel_id=1, source_target_pairs={{0,7},{1,0},{2,1},{3,2},{4,3},{5,4},{6,5},{7,6},{8,15},{9,8},{10,9... | collective-permute-start | bytes 12296 | tf_op jit(solution)/shard_map/ppermute | solution.py:367
  46.5 5.9 %collective-permute-start.2 = (f32[8,640]{1,0:T(8,128)S(1)}, f32[8,640]{1,0:T(8,128)S(1)}, u32[]{:S(2)}, u32[]{:S(2)}) collective-permute-start(f32[8,640]{1,0:T(8,128)S(1)} %get-tuple-element.27), channel_id=1, source_target_pairs={{0,8},{8,16},{16,24},{24,0},{1,9},{9,17},{17,25},{25,1},{2,10},{10... | collective-permute-start | bytes 61448 | tf_op jit(solution)/shard_map/ppermute | solution.py:367
  50.5 3.2 %collective-permute-start.3 = (f32[8,640]{1,0:T(8,128)S(1)}, f32[8,640]{1,0:T(8,128)S(1)}, u32[]{:S(2)}, u32[]{:S(2)}) collective-permute-start(f32[8,640]{1,0:T(8,128)S(1)} %get-tuple-element.28), channel_id=1, source_target_pairs={{0,24},{8,0},{16,8},{24,16},{1,25},{9,1},{17,9},{25,17},{2,26},{10... | collective-permute-start | bytes 61448 | tf_op jit(solution)/shard_map/ppermute | solution.py:367
where the time goes:
time: 55.9 us; the launch traced here: 54.9 us
  blocking collectives  26.8 us (48%)
  Pallas kernels  20.1 us (36%)
  starting transfers between devices  6.46 us (12%)
  waiting for transfers between devices  1.41 us (3%)
    all_to_all x1, blocking collectives, body(): parts = lax.all_to_all(parts, 'col', 0, 0, tiled=True)  17.6 us
    all_to_all x1, blocking collectives, body(): sums = lax.all_to_all(sums, 'col', 0, 0, tiled=True)  9.24 us
    pallas_call x1, Pallas kernels, body(): pl.pallas_call(functools.partial(outer_kernel, first_slot), out_shape=(ja...  8.72 us
    ppermute x4, starting transfers between devices, shift(): lax.ppermute(values, axis, [(i, (i + step) % count) for i in range(count)])  6.46 us
    pallas_call x1, Pallas kernels, body(): pl.pallas_call(functools.partial(inner_kernel, first_slot), out_shape=jax...  5.73 us
    pallas_call x1, Pallas kernels, body(): pl.pallas_call(functools.partial(middle_kernel, row_count, col_count), ou...  1.8 us
    pallas_call x1, Pallas kernels, body(): pl.pallas_call(pack_kernel, out_shape=(jax.ShapeDtypeStruct((col_count, f...  1.77 us
    ppermute x4, waiting for transfers between devices, shift(): lax.ppermute(values, axis, [(i, (i + step) % count) for i in range(count)])  1.41 us
  transfers between devices with their start and end apart: 4, of which 1 were waited for; matrix products, arithmetic and copies ran while one was open for 0% of the time, Pallas kernels for 14%

commit v1 on v0

--- a/solution.py
+++ b/solution.py
@@ -334,9 +334,14 @@
     out_ref[...] = height[:, :tile_columns]
 
 
-def band_kernel(row_count, col_count, height_ref, land_ref, above_ref, below_ref, _, out_hbm, rows_ref, sems):
+def band_kernel(
+    row_count, col_count, height_ref, land_ref, above_ref, below_ref, middle_ref, out_hbm, rows_ref, sems
+):
     tile_rows, tile_columns = out_hbm.shape
     keep = 16 - SWEEPS
+    middle = pl.ds(8, tile_rows - 16)
+    middle_copy = pltpu.make_async_copy(middle_ref.at[middle, :], out_hbm.at[middle, :], sems.at[2])
+    middle_copy.start()
 
     def bands(ref, k):
         halo = slice(k * SWEEPS, (k + 1) * SWEEPS)
@@ -360,6 +365,7 @@
         copy.start()
     for copy in copies:
         copy.wait()
+    middle_copy.wait()
 
 
 def shift(values, axis, step):
@@ -486,10 +492,9 @@
     return pl.pallas_call(
         functools.partial(band_kernel, row_count, col_count),
         out_shape=tile,
-        in_specs=[vmem()] * 4 + [hbm],
+        in_specs=[vmem()] * 5,
         out_specs=hbm,
-        input_output_aliases={4: 0},
-        scratch_shapes=[pltpu.VMEM((2, 8, tile_columns), F32), pltpu.SemaphoreType.DMA((2,))],
+        scratch_shapes=[pltpu.VMEM((2, 8, tile_columns), F32), pltpu.SemaphoreType.DMA((3,))],
         compiler_params=params(),
     )(height, land, from_above, from_below, depth)
 

time: 55.9 us -> 56.5 us (1.011)
  the two profiles are of different devices: /device:TPU:9 before, /device:TPU:1 now
where the time goes in v1:
time: 56.5 us
  blocking collectives  29.3 us (52%)
  Pallas kernels  15.8 us (28%)
  starting transfers between devices  9.23 us (16%)
  waiting for transfers between devices  2.1 us (4%)
    all_to_all x1, blocking collectives, body(): parts = lax.all_to_all(parts, 'col', 0, 0, tiled=True)  19.2 us
    all_to_all x1, blocking collectives, body(): sums = lax.all_to_all(sums, 'col', 0, 0, tiled=True)  10.1 us
    ppermute x4, starting transfers between devices, shift(): lax.ppermute(values, axis, [(i, (i + step) % count) for i in range(count)])  9.23 us
    pallas_call x1, Pallas kernels, body(): pl.pallas_call(functools.partial(outer_kernel, first_slot), out_shape=(ja...  6.42 us
    pallas_call x1, Pallas kernels, body(): pl.pallas_call(functools.partial(inner_kernel, first_slot), out_shape=jax...  4.46 us
    ppermute x4, waiting for transfers between devices, shift(): lax.ppermute(values, axis, [(i, (i + step) % count) for i in range(count)])  2.1 us
    pallas_call x1, Pallas kernels, body(): pl.pallas_call(pack_kernel, out_shape=(jax.ShapeDtypeStruct((col_count, f...  1.77 us
    pallas_call x1, Pallas kernels, body(): pl.pallas_call(functools.partial(band_kernel, row_count, col_count), out_...  1.15 us
  transfers between devices with their start and end apart: 4, of which 1 were waited for; matrix products, arithmetic and copies ran while one was open for 0% of the time, Pallas kernels for 10%

profile of v1, /device:TPU:1, one launch (start us, length us, event | category | flops | bytes accessed | tf_op | source)
XLA Modules:
  0.0 56.5 jit_solution(17721019021990396713)
XLA Ops:
  0.0 1.8 %shard_map.55 = (f32[8,120,128]{2,1,0:T(8,128)S(1)}, f32[128,512]{1,0:T(8,128)S(1)}, s32[2,16]{1,0:T(2,128)S(1)}) custom-call(s32[2,16]{1,0:T(2,128)} %bitcast.3, s32[8,128]{1,0:T(8,128)} %bitcast.2, f32[1024,128]{1,0:T(8,128)} %entry_hbm.1, f32[16,2,512]{2,1,0:T(2,128)} %place_hbm.1, f32[128,512]{1,0:T(8,128)} %ground_hbm.1), custom_call_target="tpu_custom_call" | custom-call | tf_op jit(solution)/shard_map/pallas_call | solution.py:392
  1.8 19.2 %all_to_all.10.part_ref.place_ref = f32[8,120,128]{2,1,0:T(8,128)S(1)} all-to-all(f32[8,120,128]{2,1,0:T(8,128)S(1)} %get-tuple-element.17), channel_id=1, replica_groups=mesh['row'=4,'col'=8] {'col'}, dimensions={0} | all-to-all | bytes 983040 | tf_op jit(solution)/shard_map/all_to_all | solution.py:422
  20.9 0.7 %shard_map.56 = f32[8,32,128]{2,1,0:T(8,128)S(1)} custom-call(s32[2,16]{1,0:T(2,128)S(1)} %get-tuple-element.18.cover_ref, f32[8,120,128]{2,1,0:T(8,128)S(1)} %all_to_all.10.part_ref.place_ref), custom_call_target="tpu_custom_call" | custom-call | tf_op jit(solution)/shard_map/pallas_call | solution.py:425
  21.7 10.1 %all_to_all.11.sums_ref = f32[8,32,128]{2,1,0:T(8,128)S(1)} all-to-all(f32[8,32,128]{2,1,0:T(8,128)S(1)} %shard_map.56), channel_id=1, replica_groups=mesh['row'=4,'col'=8] {'col'}, dimensions={0} | all-to-all | bytes 262144 | tf_op jit(solution)/shard_map/all_to_all | solution.py:436
  31.8 6.4 %shard_map.57 = (f32[128,256]{1,0:T(8,128)S(1)}, f32[8,128]{1,0:T(8,128)S(1)}, f32[8,128]{1,0:T(8,128)S(1)}, bf16[192,256,128]{2,1,0:T(8,128)(2,1)S(1)}, f32[8,128]{1,0:T(8,128)S(1)}) custom-call(f32[8,120,128]{2,1,0:T(8,128)S(1)} %all_to_all.10.part_ref.place_ref, f32[8,32,128]{2,1,0:T(8,128)S(1)} %all_to_all.11.sums_ref, ...), custom_call_target="tpu_custom_call" | custom-call | flops 3221225472 | bytes 1048576 | tf_op jit(solution)/shard_map/pallas_call | solution.py:442
  38.2 0.1 collective-permute-start
  38.3 4.1 %collective-permute-start.1 = (f32[8,128]{1,0:T(8,128)S(1)}, f32[8,128]{1,0:T(8,128)S(1)}, u32[]{:S(2)}, u32[]{:S(2)}) collective-permute-start(f32[8,128]{1,0:T(8,128)S(1)} %get-tuple-element.24), channel_id=1, source_target_pairs={{0,7},{1,0},{2,1},{3,2},{4,3},{5,4},{6,5},{7,6},{8,15},{9,8},{10,9... | collective-permute-start | bytes 12296 | tf_op jit(solution)/shard_map/ppermute | solution.py:373
  42.4 4.5 %shard_map.58.inner_ref = f32[128,256]{1,0:T(8,128)S(1)} custom-call(f32[8,120,128]{2,1,0:T(8,128)S(1)} %all_to_all.10.part_ref.place_ref, bf16[192,256,128]{2,1,0:T(8,128)(2,1)S(1)} %get-tuple-element.21.stack_ref, f32[8,128]{1,0:T(8,128)S(1)} %get-tuple-element.22.mean_ref, f32[128,512]{1,0:T(8,128)S(1)} %get-tuple-element.19.ground_ref), custom_call_target="tpu_custom_call" | custom-call | flops 3221225472 | bytes 1048576 | tf_op jit(solution)/shard_map/pallas_call | solution.py:460
  46.9 0.0 collective-permute-done.left_ref
  46.9 0.0 collective-permute-done.1.right_ref
  46.9 0.2 shard_map.59
  47.1 5.0 %collective-permute-start.2 = (f32[8,640]{1,0:T(8,128)S(1)}, f32[8,640]{1,0:T(8,128)S(1)}, u32[]{:S(2)}, u32[]{:S(2)}) collective-permute-start(f32[8,640]{1,0:T(8,128)S(1)} %get-tuple-element.27), channel_id=1, source_target_pairs={{0,8},{8,16},{16,24},{24,0},{1,9},{9,17},{17,25},{25,1},{2,10},{10... | collective-permute-start | bytes 61448 | tf_op jit(solution)/shard_map/ppermute | solution.py:373
  52.2 0.0 collective-permute-start.3
  52.2 1.1 %shard_map.60.middle_ref = f32[128,512]{1,0:T(8,128)S(1)} custom-call(f32[128,640]{1,0:T(8,128)S(1)} %get-tuple-element.25.height_ref, f32[128,640]{1,0:T(8,128)S(1)} %get-tuple-element.26.land_ref), custom_call_target="tpu_custom_call" | custom-call | flops 6553600 | bytes 4194304 | tf_op jit(solution)/shard_map/pallas_call | solution.py:482
  53.3 0.0 collective-permute-done.2.above_ref
  53.3 2.1 %collective-permute-done.3.below_ref = f32[8,640]{1,0:T(8,128)S(1)} collective-permute-done((f32[8,640]{1,0:T(8,128)S(1)}, f32[8,640]{1,0:T(8,128)S(1)}, u32[]{:S(2)}, u32[]{:S(2)}) %collective-permute-start.3) | collective-permute-done | bytes 20512 | tf_op jit(solution)/shard_map/ppermute | solution.py:373
  55.4 1.1 %shard_map.61 = f32[128,512]{1,0:T(8,128)} custom-call(f32[128,640]{1,0:T(8,128)S(1)} %get-tuple-element.25.height_ref, f32[128,640]{1,0:T(8,128)S(1)} %get-tuple-element.26.land_ref, f32[8,640]{1,0:T(8,128)S(1)} %collective-permute-done.2.above_ref, f32[8,640]{1,0:T(8,128)S(1)} %collective-permute-done.3.below_ref, f32[128,512]{1,0:T(8,128)S(1)} %shard_map.60.middle_ref), custom_call_target="tpu_custom_call" | custom-call | tf_op jit(solution)/shard_map/pallas_call | solution.py:492
Async XLA Ops:
  38.2 8.7 %collective-permute-start = (f32[8,128]{1,0:T(8,128)S(1)}, f32[8,128]{1,0:T(8,128)S(1)}, u32[]{:S(2)}, u32[]{:S(2)}) collective-permute-start(f32[8,128]{1,0:T(8,128)S(1)} %get-tuple-element.23), channel_id=1, source_target_pairs={{0,1},{1,2},{2,3},{3,4},{4,5},{5,6},{6,7},{7,0},{8,9},{9,10},{10,1... | collective-permute-start | bytes 12296 | tf_op jit(solution)/shard_map/ppermute | solution.py:373
  38.3 8.6 %collective-permute-start.1 = (f32[8,128]{1,0:T(8,128)S(1)}, f32[8,128]{1,0:T(8,128)S(1)}, u32[]{:S(2)}, u32[]{:S(2)}) collective-permute-start(f32[8,128]{1,0:T(8,128)S(1)} %get-tuple-element.24), channel_id=1, source_target_pairs={{0,7},{1,0},{2,1},{3,2},{4,3},{5,4},{6,5},{7,6},{8,15},{9,8},{10,9... | collective-permute-start | bytes 12296 | tf_op jit(solution)/shard_map/ppermute | solution.py:373
  47.1 6.1 %collective-permute-start.2 = (f32[8,640]{1,0:T(8,128)S(1)}, f32[8,640]{1,0:T(8,128)S(1)}, u32[]{:S(2)}, u32[]{:S(2)}) collective-permute-start(f32[8,640]{1,0:T(8,128)S(1)} %get-tuple-element.27), channel_id=1, source_target_pairs={{0,8},{8,16},{16,24},{24,0},{1,9},{9,17},{17,25},{25,1},{2,10},{10... | collective-permute-start | bytes 61448 | tf_op jit(solution)/shard_map/ppermute | solution.py:373
  52.2 3.2 %collective-permute-start.3 = (f32[8,640]{1,0:T(8,128)S(1)}, f32[8,640]{1,0:T(8,128)S(1)}, u32[]{:S(2)}, u32[]{:S(2)}) collective-permute-start(f32[8,640]{1,0:T(8,128)S(1)} %get-tuple-element.28), channel_id=1, source_target_pairs={{0,24},{8,0},{16,8},{24,16},{1,25},{9,1},{17,9},{25,17},{2,26},{10... | collective-permute-start | bytes 61448 | tf_op jit(solution)/shard_map/ppermute | solution.py:373
